TPU v7x, 256 devices: a whole 4x4x8 slice. The times are simulated.
256 devices in a mesh: wide: 32 (over z, y), slab: 8 (over x, core).
Axes of the slice: x: 4, y: 4, z: 8, core: 2. Of those that a mesh axis runs over, the one named last changes fastest.
Arguments:
- thermal_state: float32 [32, 128, 32, 1024], P('wide', 'slab'), may hold values from -5 to 5
- thermal_spreading_rate: bfloat16 [32, 128, 32, 1024], P('wide', 'slab'), may hold values from 0.5 to 1.5
- flow_speed_vector: bfloat16 [3, 32, 128, 32, 1024], P(None, 'wide', 'slab'), may hold values from -0.796875 to 0.796875
- interface_guess: float32 [32, 2048], P('wide', 'slab'), may hold values from -4 to 4
- partner_facing_rows: int32 [32, 2048], P('wide', 'slab'), may hold values from 0 to 2047, each once within a row
- mismatch_change_matrix: float32 [32, 2048, 128], P('wide', 'slab'), may hold values from -5 to 5
- output_change_matrix: float32 [32, 2048, 128], P('wide', 'slab'), may hold values from -1.8 to 1.8
Outputs:
- temperature_out: float32 [32, 128, 32, 1024], P('wide', 'slab')
- updated_interface_guess: float32 [32, 2048], P('wide', 'slab')
- unitary_basis_factor: float32 [32, 2048, 128], P('wide', 'slab')
Inputs may be any that keep to these rules, and one draw needn't show every extreme that they name: `partner_facing_rows`: each partition's rows of matching are a permutation of its partner's interface rows.
All inputs are finite; a program needn't handle non-finite values.
Results may differ from a plain program's by a relative error of at most 0.0003.
Values may be sent and summed in bfloat16 or wider, within the bound.
No kernel may reach another device: no remote copies, remote signals or barrier semaphores. Data moves between devices by JAX's collectives and lax.ppermute only.
A program may use at most 64 MiB of HBM per device.

v0:
```python
import math
import jax
import jax.numpy as jnp
from jax import lax
from jax.sharding import PartitionSpec as P

INTERFACE_STRIP = 64
SWEEPS = 4
STEP_SIZE = 0.11


def padded(cells, sides, width):
    for axis, dim in sides:
        count = lax.axis_size(axis)
        ends = count - 1
        head = lax.slice_in_dim(cells, 0, width, axis=dim)
        tail = lax.slice_in_dim(cells, cells.shape[dim] - width, cells.shape[dim], axis=dim)
        cells = jnp.concatenate(
            [
                lax.ppermute(tail, axis, [(i, (i + 1) % count) for i in range(ends)]),
                cells,
                lax.ppermute(head, axis, [((i + 1) % count, i) for i in range(ends)]),
            ],
            axis=dim,
        )
    return cells


def partner(value, axis, stride):
    mask = 2**stride
    pairs = [(source, source ^ mask) for source in range(lax.axis_size(axis))]
    return lax.ppermute(value, axis, pairs)


def surround_wrapper(block_rows, mirror_layer):
    bottom = jnp.zeros((block_rows.shape[0], 1, block_rows.shape[2]), block_rows.dtype)
    stacked = jnp.concatenate([bottom, block_rows, mirror_layer[:, None, :]], axis=1)
    return jnp.pad(stacked, ((0, 0), (0, 0), (1, 1)))


def march_forward(bordered_array, diffuse_subdomain, subdomain_flow_speed):
    centre = bordered_array[1:-1, 1:-1, 1:-1]
    plus_first = bordered_array[2:, 1:-1, 1:-1]
    minus_first = bordered_array[:-2, 1:-1, 1:-1]
    plus_second = bordered_array[1:-1, 2:, 1:-1]
    minus_second = bordered_array[1:-1, :-2, 1:-1]
    plus_third = bordered_array[1:-1, 1:-1, 2:]
    minus_third = bordered_array[1:-1, 1:-1, :-2]
    spread = (
        plus_first
        + minus_first
        + plus_second
        + minus_second
        + plus_third
        + minus_third
        - 6.0 * centre
    )
    carried = 0.5 * (
        subdomain_flow_speed[0].astype(jnp.float32) * (plus_first - minus_first)
        + subdomain_flow_speed[1].astype(jnp.float32) * (plus_second - minus_second)
        + subdomain_flow_speed[2].astype(jnp.float32) * (plus_third - minus_third)
    )
    return centre + STEP_SIZE * (diffuse_subdomain.astype(jnp.float32) * spread - carried)


def shards(
    thermal_state,
    thermal_spreading_rate,
    flow_speed_vector,
    interface_guess,
    partner_facing_rows,
    mismatch_change_matrix,
    output_change_matrix,
):
    subdomain_thermal_state = thermal_state[0]
    diffuse_subdomain = thermal_spreading_rate[0]
    subdomain_flow_speed = flow_speed_vector[:, 0]
    layer_stack = subdomain_thermal_state.shape[0]
    vertical_extent = subdomain_thermal_state.shape[1]
    rows_dev = interface_guess.shape[1]
    mirror_layer = jnp.repeat(interface_guess[0].reshape(layer_stack, -1), INTERFACE_STRIP, axis=1)
    panel = mismatch_change_matrix[0]
    gram_local = lax.dot_general(
        panel,
        panel,
        (((0,), (0,)), ((), ())),
        precision=lax.Precision.HIGHEST,
        preferred_element_type=jnp.float32,
    )
    ghost_padded = jnp.pad(mirror_layer, ((1, 1), (0, 0)))
    for sweep in range(SWEEPS):
        widened_array = padded(subdomain_thermal_state, (("slab", 0),), 1)
        subdomain_thermal_state = march_forward(
            surround_wrapper(widened_array, ghost_padded), diffuse_subdomain, subdomain_flow_speed
        )
    face_means = jnp.mean(
        subdomain_thermal_state[:, vertical_extent - 1, :].reshape(
            layer_stack, -1, INTERFACE_STRIP
        ),
        axis=2,
    )
    face_means = face_means.reshape(1, rows_dev)
    top_bit = lax.axis_size("wide").bit_length() - 2
    partner_own = partner(face_means, "wide", top_bit)
    partner_all = lax.all_gather(partner_own, "slab", axis=1, tiled=True)
    tilde = jnp.take(partner_all[0], partner_facing_rows[0], axis=0)
    resid = tilde - interface_guess[0]
    proj_local = jnp.dot(
        resid, panel, precision=lax.Precision.HIGHEST, preferred_element_type=jnp.float32
    )
    gram_matrix, projection = lax.psum((gram_local, proj_local), ("wide", "slab"))
    lower_factor = jnp.linalg.cholesky(gram_matrix)
    half_solve = lax.linalg.triangular_solve(
        lower_factor, projection[:, None], left_side=True, lower=True
    )
    coefficients = -lax.linalg.triangular_solve(
        lower_factor, half_solve, left_side=True, lower=True, transpose_a=True
    )[:, 0]
    update = jnp.dot(
        output_change_matrix[0],
        coefficients,
        precision=lax.Precision.HIGHEST,
        preferred_element_type=jnp.float32,
    )
    updated_interface_guess = tilde + update
    total_rows = rows_dev * lax.axis_size("slab") * lax.axis_size("wide")
    scaled = lax.linalg.triangular_solve(
        lower_factor, panel, left_side=False, lower=True, transpose_a=True
    )
    unitary_basis_factor = math.sqrt(total_rows) * scaled
    return (
        subdomain_thermal_state[None],
        updated_interface_guess[None],
        unitary_basis_factor[None],
    )


def solution(mesh):
    return jax.shard_map(
        shards,
        mesh=mesh,
        in_specs=(
            P("wide", "slab", None, None),
            P("wide", "slab", None, None),
            P(None, "wide", "slab", None, None),
            P("wide", "slab"),
            P("wide", "slab"),
            P("wide", "slab", None),
            P("wide", "slab", None),
        ),
        out_specs=(P("wide", "slab", None, None), P("wide", "slab"), P("wide", "slab", None)),
        check_vma=False,
    )
```

profile of v0, /device:TPU:1, one launch (start us, length us, event | category | flops | bytes accessed | tf_op | source)
XLA Modules:
  0.0 438.8 jit_solution(339822084845978649)
XLA Ops:
  8.2 5.1 %collective-permute-start = (f32[1,32,1024]{2,1,0:T(8,128)S(1)}, f32[1,32,1024]{2,1,0:T(8,128)S(1)}, u32[]{:S(2)}, u32[]{:S(2)}) collective-permute-start(f32[1,32,1024]{2,1,0:T(8,128)S(1)} %get-tuple-element.16), channel_id=1, source_target_pairs={{1,0},{2,1},{3,2},{4,3},{5,4},{6,5},{7,6},{9,8},{10,9},{11,10},{12... | collective-permute-start | bytes 393224 | tf_op jit(solution)/shard_map/ppermute | solution.py:22
  13.4 1.9 collective-permute-start.1
  17.6 1.3 reduce.11
  19.3 237.0 %all-reduce.11.cloned.1.call-done = f32[128,128]{0,1:T(8,128)} async-done(((f32[128,128]{0,1:T(8,128)}), f32[128,128]{0,1:T(8,128)}) %all-reduce.11.cloned.1.call-update) | async-done | bytes 65552 | tf_op jit(solution)/shard_map/psum | solution.py:111
  257.9 2.3 pad_maximum_fusion.3
  260.7 7.0 %fusion.2 = f32[16,32,1024]{2,1,0:T(8,128)S(1)} fusion(f32[16,32,1024]{2,1,0:T(8,128)} %bitcast.90, f32[18,34,1024]{2,1,0:T(8,128)S(1)} %pad_maximum_fusion.3, f32[1,32,1024]{2,1,0:T(8,128)S(1)} %collective-permute-done, f32[1,32,1024]{2,1,0:T(8,128)S(1)} %copy-done.11, f32[18,1,1024]{2,1,0:T(1,128)S(1)} %broadcast_in_dim.30, ...), kind=kLoop, calls=%fused_computation.35 | loop fusion | flops 18874368 | bytes 11231232 | tf_op jit(solution)/shard_map/add | solution.py:63
  267.8 1.3 copy-done.4
  269.8 1.9 collective-permute-start.2
  271.7 3.6 collective-permute-start.3
  276.0 12.5 %cholesky.16 = f32[128,128]{1,0:T(8,128)S(1)} custom-call(f32[128,128]{1,0:T(8,128)} %fusion.45), custom_call_target="Cholesky" | custom-call | tf_op jit(solution)/shard_map/jit(cholesky)/cholesky | solution.py:112
  288.6 2.3 pad_maximum_fusion.2
  291.1 4.6 %fusion.5 = f32[16,32,1024]{2,1,0:T(8,128)S(1)} fusion(f32[16,32,1024]{2,1,0:T(8,128)S(1)} %copy-done.5, f32[18,34,1024]{2,1,0:T(8,128)S(1)} %pad_maximum_fusion.2, f32[1,32,1024]{2,1,0:T(8,128)S(1)} %collective-permute-done.2, f32[1,32,1024]{2,1,0:T(8,128)} %collective-permute-done.3, f32[18,1,1024]{2,1,0:T(1,128)S(1)} %broadcast_in_dim.30, ...), kind=kLoop, calls=%fused_computation.38 | loop fusion | flops 18874368 | bytes 11231232 | tf_op jit(solution)/shard_map/add | solution.py:63
  295.8 1.9 collective-permute-start.4
  297.7 3.8 collective-permute-start.5
  304.0 5.4 %fusion.8 = f32[16,32,1024]{2,1,0:T(8,128)S(1)} fusion(f32[16,32,1024]{2,1,0:T(8,128)S(1)} %fusion.5, f32[18,34,1024]{2,1,0:T(8,128)S(1)} %pad_maximum_fusion.1, f32[1,32,1024]{2,1,0:T(8,128)S(1)} %collective-permute-done.4, f32[1,32,1024]{2,1,0:T(8,128)S(1)} %collective-permute-done.5, f32[18,1,1024]{2,1,0:T(1,128)S(1)} %broadcast_in_dim.30, ...), kind=kLoop, calls=%fused_computation.41 | loop fusion | flops 18874368 | bytes 11231232 | tf_op jit(solution)/shard_map/add | solution.py:63
  311.4 1.9 collective-permute-start.6
  313.3 4.4 collective-permute-start.7
  319.0 10.6 %custom-call.10 = f32[1,128,128]{1,2,0:T(8,128)S(1)} custom-call(f32[1,128,128]{2,1,0:T(8,128)} %fusion.41), custom_call_target="InvertDiagBlocksLowerTriangular" | custom-call | tf_op jit(solution)/shard_map/triangular_solve | solution.py:116
  329.7 2.3 pad_maximum_fusion
  332.2 4.6 %fusion.11 = f32[16,32,1024]{2,1,0:T(8,128)S(1)} fusion(f32[16,32,1024]{2,1,0:T(8,128)S(1)} %copy-done.3, f32[18,34,1024]{2,1,0:T(8,128)S(1)} %pad_maximum_fusion, f32[1,32,1024]{2,1,0:T(8,128)S(1)} %collective-permute-done.6, f32[1,32,1024]{2,1,0:T(8,128)} %collective-permute-done.7, f32[18,1,1024]{2,1,0:T(1,128)S(1)} %broadcast_in_dim.30, ...), kind=kLoop, calls=%fused_computation.44 | loop fusion | flops 18874368 | bytes 11231232 | tf_op jit(solution)/shard_map/add | solution.py:63
  340.6 4.4 %collective-permute-done.8 = f32[1,256]{1,0:T(1,128)S(1)} collective-permute-done((f32[1,256]{1,0:T(1,128)S(1)}, f32[1,256]{1,0:T(1,128)S(1)}, u32[]{:S(2)}, u32[]{:S(2)}) %collective-permute-start.8) | collective-permute-done | bytes 1056 | tf_op jit(solution)/shard_map/ppermute | solution.py:32
  345.0 10.1 %all_gather.3 = f32[1,2048]{1,0:T(1,128)S(1)} all-gather(f32[1,256]{1,0:T(1,128)S(1)} %collective-permute-done.8), channel_id=1, replica_groups=mesh['wide'=32,'slab'=8] {'slab'}, dimensions={1}, use_global_device_ids=true | all-gather | bytes 9216 | tf_op jit(solution)/shard_map/all_gather | solution.py:105
  355.1 1.7 gather_fusion
  357.0 73.7 %psum.15 = f32[128]{0:T(128)S(1)} all-reduce(f32[128]{0:T(128)S(1)} %convolution_bitcast_fusion.2), channel_id=1, replica_groups=mesh['wide'=32,'slab'=8] {'wide','slab'}, use_global_device_ids=true, to_apply=%region_4.5 | all-reduce | flops 128 | bytes 1024 | tf_op jit(solution)/shard_map/psum | solution.py:111
  (78 shorter events, 18.4 us)
Async XLA Ops:
  7.2 8.2 %copy-start = (f32[1,256,128]{2,1,0:T(8,128)S(1)}, f32[1,256,128]{2,1,0:T(8,128)}, u32[]{:S(2)}) copy-start(f32[1,256,128]{2,1,0:T(8,128)} %param.12) | copy-start | bytes 393220
  7.2 249.1 %all-reduce.11.cloned.1.call-start = ((), (), s32[]{:S(2)}) async-start(), calls=%async_computation | async-start | bytes 131072 | tf_op jit(solution)/shard_map/psum | solution.py:111
  8.2 249.0 %collective-permute-start = (f32[1,32,1024]{2,1,0:T(8,128)S(1)}, f32[1,32,1024]{2,1,0:T(8,128)S(1)}, u32[]{:S(2)}, u32[]{:S(2)}) collective-permute-start(f32[1,32,1024]{2,1,0:T(8,128)S(1)} %get-tuple-element.16), channel_id=1, source_target_pairs={{1,0},{2,1},{3,2},{4,3},{5,4},{6,5},{7,6},{9,8},{10,9},{11,10},{12... | collective-permute-start | bytes 393224 | tf_op jit(solution)/shard_map/ppermute | solution.py:22
  13.4 243.8 %collective-permute-start.1 = (f32[1,32,1024]{2,1,0:T(8,128)S(1)}, f32[1,32,1024]{2,1,0:T(8,128)S(1)}, u32[]{:S(2)}, u32[]{:S(2)}) collective-permute-start(f32[1,32,1024]{2,1,0:T(8,128)S(1)} %get-tuple-element.15), channel_id=1, source_target_pairs={{0,1},{1,2},{2,3},{3,4},{4,5},{5,6},{6,7},{8,9},{9,10},{10,11},{11... | collective-permute-start | bytes 393224 | tf_op jit(solution)/shard_map/ppermute | solution.py:20
  257.9 2.6 copy-start.1
  257.9 2.8 copy-start.6
  257.9 2.8 copy-start.11
  260.7 14.6 %copy-start.12 = (f32[128,128]{0,1:T(8,128)S(1)}, f32[128,128]{0,1:T(8,128)}, u32[]{:S(2)}) copy-start(f32[128,128]{0,1:T(8,128)} %all-reduce.11.cloned.1.call-done) | copy-start | bytes 196612
  269.8 18.8 %collective-permute-start.2 = (f32[1,32,1024]{2,1,0:T(8,128)}, f32[1,32,1024]{2,1,0:T(8,128)S(1)}, u32[]{:S(2)}, u32[]{:S(2)}) collective-permute-start(f32[1,32,1024]{2,1,0:T(8,128)} %get-tuple-element.14), channel_id=1, source_target_pairs={{1,0},{2,1},{3,2},{4,3},{5,4},{6,5},{7,6},{9,8},{10,9},{11,10},{12... | collective-permute-start | bytes 393224 | tf_op jit(solution)/shard_map/ppermute | solution.py:22
  271.7 16.9 %collective-permute-start.3 = (f32[1,32,1024]{2,1,0:T(8,128)}, f32[1,32,1024]{2,1,0:T(8,128)}, u32[]{:S(2)}, u32[]{:S(2)}) collective-permute-start(f32[1,32,1024]{2,1,0:T(8,128)} %get-tuple-element.13), channel_id=1, source_target_pairs={{0,1},{1,2},{2,3},{3,4},{4,5},{5,6},{6,7},{8,9},{9,10},{10,11},{11... | collective-permute-start | bytes 393224 | tf_op jit(solution)/shard_map/ppermute | solution.py:20
  288.6 13.0 %copy-start.13 = (f32[128,128]{1,0:T(8,128)}, f32[128,128]{1,0:T(8,128)S(1)}, u32[]{:S(2)}) copy-start(f32[128,128]{1,0:T(8,128)S(1)} %cholesky.16) | copy-start | bytes 196612
  288.6 2.3 copy-start.5
  288.6 2.5 copy-start.7
  295.8 6.4 %collective-permute-start.4 = (f32[1,32,1024]{2,1,0:T(8,128)S(1)}, f32[1,32,1024]{2,1,0:T(8,128)S(1)}, u32[]{:S(2)}, u32[]{:S(2)}) collective-permute-start(f32[1,32,1024]{2,1,0:T(8,128)S(1)} %get-tuple-element.12), channel_id=1, source_target_pairs={{1,0},{2,1},{3,2},{4,3},{5,4},{6,5},{7,6},{9,8},{10,9},{11,10},{12... | collective-permute-start | bytes 393224 | tf_op jit(solution)/shard_map/ppermute | solution.py:22
  297.7 5.6 %collective-permute-start.5 = (f32[1,32,1024]{2,1,0:T(8,128)S(1)}, f32[1,32,1024]{2,1,0:T(8,128)S(1)}, u32[]{:S(2)}, u32[]{:S(2)}) collective-permute-start(f32[1,32,1024]{2,1,0:T(8,128)S(1)} %get-tuple-element.11), channel_id=1, source_target_pairs={{0,1},{1,2},{2,3},{3,4},{4,5},{5,6},{6,7},{8,9},{9,10},{10,11},{11... | collective-permute-start | bytes 393224 | tf_op jit(solution)/shard_map/ppermute | solution.py:20
  304.0 13.7 %copy-start.14 = (f32[128,128]{1,0:T(8,128)S(1)}, f32[128,128]{1,0:T(8,128)}, u32[]{:S(2)}) copy-start(f32[128,128]{1,0:T(8,128)} %copy-done.13) | copy-start | bytes 196612
  311.4 18.2 %collective-permute-start.6 = (f32[1,32,1024]{2,1,0:T(8,128)}, f32[1,32,1024]{2,1,0:T(8,128)S(1)}, u32[]{:S(2)}, u32[]{:S(2)}) collective-permute-start(f32[1,32,1024]{2,1,0:T(8,128)} %get-tuple-element.10), channel_id=1, source_target_pairs={{1,0},{2,1},{3,2},{4,3},{5,4},{6,5},{7,6},{9,8},{10,9},{11,10},{12... | collective-permute-start | bytes 393224 | tf_op jit(solution)/shard_map/ppermute | solution.py:22
  313.3 16.3 %collective-permute-start.7 = (f32[1,32,1024]{2,1,0:T(8,128)}, f32[1,32,1024]{2,1,0:T(8,128)}, u32[]{:S(2)}, u32[]{:S(2)}) collective-permute-start(f32[1,32,1024]{2,1,0:T(8,128)} %get-tuple-element.9), channel_id=1, source_target_pairs={{0,1},{1,2},{2,3},{3,4},{4,5},{5,6},{6,7},{8,9},{9,10},{10,11},{11... | collective-permute-start | bytes 393224 | tf_op jit(solution)/shard_map/ppermute | solution.py:20
  329.6 2.3 copy-start.3
  329.7 2.5 copy-start.8
  338.2 18.6 %copy-start.16 = (s32[1,256]{1,0:T(1,128)S(1)}, s32[1,256]{1,0:T(1,128)}, u32[]{:S(2)}) copy-start(s32[1,256]{1,0:T(1,128)} %param.11) | copy-start | bytes 3076
  338.2 18.6 %copy-start.17 = (f32[1,256]{1,0:T(1,128)S(1)}, f32[1,256]{1,0:T(1,128)}, u32[]{:S(2)}) copy-start(f32[1,256]{1,0:T(1,128)} %param.10) | copy-start | bytes 3076
  338.2 92.9 %copy-start.15 = (f32[1,256,128]{2,1,0:T(8,128)S(1)}, f32[1,256,128]{2,1,0:T(8,128)}, u32[]{:S(2)}) copy-start(f32[1,256,128]{2,1,0:T(8,128)} %param.13) | copy-start | bytes 393220
  338.6 6.4 %collective-permute-start.8 = (f32[1,256]{1,0:T(1,128)S(1)}, f32[1,256]{1,0:T(1,128)S(1)}, u32[]{:S(2)}, u32[]{:S(2)}) collective-permute-start(f32[1,256]{1,0:T(1,128)S(1)} %div.18), channel_id=1, source_target_pairs={{0,128},{8,136},{16,144},{24,152},{32,160},{40,168},{48,176},{56,1... | collective-permute-start | bytes 3080 | tf_op jit(solution)/shard_map/ppermute | solution.py:32
  (4 other events, 4.6 us)
Sparse Core Ops, SparseCore 0:
  16.5 239.7 all-reduce.10
where the time goes:
time: 439 us
  waiting for transfers between devices  242 us (55%)
  blocking collectives  83.8 us (19%)
  other arithmetic  57.7 us (13%)
  starting transfers between devices  25.5 us (6%)
  between operations  14.5 us (3%)
  local copies, waits for them, and re-layouts  12.7 us (3%)
    psum x1, waiting for transfers between devices, shards(): lax.psum((gram_local, proj_local), ('wide', 'slab'))  237 us
    psum x1, blocking collectives, shards(): lax.psum((gram_local, proj_local), ('wide', 'slab'))  73.7 us
    add x4, other arithmetic, march_forward(): centre + STEP_SIZE * (diffuse_subdomain.astype(jnp.float32) * spread - ca...  21.7 us
    ppermute x4, starting transfers between devices, padded(): lax.ppermute(tail, axis, [(i, (i + 1) % count) for i in range(ends)])  13.7 us
    another operation x3, other arithmetic, shards(): lower_factor = jnp.linalg.cholesky(gram_matrix)  13.2 us
    another operation x2, other arithmetic, shards(): lax.linalg.triangular_solve(lower_factor, half_solve, left_side=True, low...  11.9 us
    ppermute x4, starting transfers between devices, padded(): lax.ppermute(head, axis, [((i + 1) % count, i) for i in range(ends)])  10.9 us
    all_gather x1, blocking collectives, shards(): partner_all = lax.all_gather(partner_own, 'slab', axis=1, tiled=True)  10.1 us
  transfers between devices with their start and end apart: 10, of which 3 were waited for; matrix products, arithmetic and copies ran while one was open for 7% of the time, Pallas kernels for 0%

commit v1 on v0

--- a/solution.py
+++ b/solution.py
@@ -108,7 +108,7 @@
     proj_local = jnp.dot(
         resid, panel, precision=lax.Precision.HIGHEST, preferred_element_type=jnp.float32
     )
-    gram_matrix, projection = lax.psum((gram_local, proj_local), ("wide", "slab"))
+    gram_matrix, projection = lax.psum(lax.psum((gram_local, proj_local), "slab"), "wide")
     lower_factor = jnp.linalg.cholesky(gram_matrix)
     half_solve = lax.linalg.triangular_solve(
         lower_factor, projection[:, None], left_side=True, lower=True

time: 439 us -> 416 us (0.948)
  the two profiles are of different devices: /device:TPU:1 before, /device:TPU:0 now
where the time goes in v1:
time: 416 us; the launch traced here: 415 us
  waiting for transfers between devices  209 us (50%)
  blocking collectives  97.5 us (23%)
  other arithmetic  56.3 us (14%)
  starting transfers between devices  23.4 us (6%)
  between operations  14.4 us (3%)
  local copies, waits for them, and re-layouts  12.7 us (3%)
    psum x1, waiting for transfers between devices, shards(): lax.psum(lax.psum((gram_local, proj_local), 'slab'), 'wide')  142 us
    psum x1, blocking collectives, shards(): lax.psum(lax.psum((gram_local, proj_local), 'slab'), 'wide')  72.9 us
    psum x1, waiting for transfers between devices, shards(): lax.psum((gram_local, proj_local), 'slab')  62.9 us
    add x4, other arithmetic, march_forward(): centre + STEP_SIZE * (diffuse_subdomain.astype(jnp.float32) * spread - ca...  21.7 us
    ppermute x4, starting transfers between devices, padded(): lax.ppermute(tail, axis, [(i, (i + 1) % count) for i in range(ends)])  15.8 us
    another operation x3, other arithmetic, shards(): lower_factor = jnp.linalg.cholesky(gram_matrix)  13.2 us
    psum x1, blocking collectives, shards(): lax.psum((gram_local, proj_local), 'slab')  12.7 us
    all_gather x1, blocking collectives, shards(): partner_all = lax.all_gather(partner_own, 'slab', axis=1, tiled=True)  11.8 us
  transfers between devices with their start and end apart: 11, of which 4 were waited for; matrix products, arithmetic and copies ran while one was open for 7% of the time, Pallas kernels for 0%

profile of v1, /device:TPU:0, one launch (start us, length us, event | category | flops | bytes accessed | tf_op | source)
XLA Modules:
  0.0 415.4 jit_solution(10058338562083767768)
XLA Ops:
  9.5 3.0 collective-permute-start.1
  14.9 1.3 reduce.11
  16.6 62.9 %all-reduce.12.cloned.1.call-done = f32[128,128]{0,1:T(8,128)} async-done(((f32[128,128]{0,1:T(8,128)}), f32[128,128]{0,1:T(8,128)}) %all-reduce.12.cloned.1.call-update) | async-done | bytes 65552 | tf_op jit(solution)/shard_map/psum | solution.py:111
  79.6 141.9 %all-reduce.14.cloned.1.call-done = f32[128,128]{0,1:T(8,128)} async-done(((f32[128,128]{0,1:T(8,128)}), f32[128,128]{0,1:T(8,128)}) %all-reduce.14.cloned.1.call-update) | async-done | bytes 65552 | tf_op jit(solution)/shard_map/psum | solution.py:111
  223.1 2.3 pad_maximum_fusion.3
  225.9 7.0 %fusion.2 = f32[16,32,1024]{2,1,0:T(8,128)S(1)} fusion(f32[16,32,1024]{2,1,0:T(8,128)} %bitcast.90, f32[18,34,1024]{2,1,0:T(8,128)S(1)} %pad_maximum_fusion.3, f32[1,32,1024]{2,1,0:T(8,128)S(1)} %collective-permute-done, f32[1,32,1024]{2,1,0:T(8,128)S(1)} %copy-done.11, f32[18,1,1024]{2,1,0:T(1,128)S(1)} %broadcast_in_dim.30, ...), kind=kLoop, calls=%fused_computation.35 | loop fusion | flops 18874368 | bytes 11231232 | tf_op jit(solution)/shard_map/add | solution.py:63
  232.9 1.3 copy-done.4
  236.2 3.7 collective-permute-start.3
  240.6 12.5 %cholesky.16 = f32[128,128]{1,0:T(8,128)S(1)} custom-call(f32[128,128]{1,0:T(8,128)} %fusion.45), custom_call_target="Cholesky" | custom-call | tf_op jit(solution)/shard_map/jit(cholesky)/cholesky | solution.py:112
  253.2 2.3 pad_maximum_fusion.2
  255.7 4.6 %fusion.5 = f32[16,32,1024]{2,1,0:T(8,128)S(1)} fusion(f32[16,32,1024]{2,1,0:T(8,128)S(1)} %copy-done.5, f32[18,34,1024]{2,1,0:T(8,128)S(1)} %pad_maximum_fusion.2, f32[1,32,1024]{2,1,0:T(8,128)S(1)} %collective-permute-done.2, f32[1,32,1024]{2,1,0:T(8,128)} %collective-permute-done.3, f32[18,1,1024]{2,1,0:T(1,128)S(1)} %broadcast_in_dim.30, ...), kind=kLoop, calls=%fused_computation.38 | loop fusion | flops 18874368 | bytes 11231232 | tf_op jit(solution)/shard_map/add | solution.py:63
  261.6 3.2 collective-permute-start.5
  266.3 5.4 %fusion.8 = f32[16,32,1024]{2,1,0:T(8,128)S(1)} fusion(f32[16,32,1024]{2,1,0:T(8,128)S(1)} %fusion.5, f32[18,34,1024]{2,1,0:T(8,128)S(1)} %pad_maximum_fusion.1, f32[1,32,1024]{2,1,0:T(8,128)S(1)} %collective-permute-done.4, f32[1,32,1024]{2,1,0:T(8,128)S(1)} %collective-permute-done.5, f32[18,1,1024]{2,1,0:T(1,128)S(1)} %broadcast_in_dim.30, ...), kind=kLoop, calls=%fused_computation.41 | loop fusion | flops 18874368 | bytes 11231232 | tf_op jit(solution)/shard_map/add | solution.py:63
  271.7 1.3 copy-done.2
  275.1 5.8 %collective-permute-start.7 = (f32[1,32,1024]{2,1,0:T(8,128)}, f32[1,32,1024]{2,1,0:T(8,128)}, u32[]{:S(2)}, u32[]{:S(2)}) collective-permute-start(f32[1,32,1024]{2,1,0:T(8,128)} %get-tuple-element.9), channel_id=1, source_target_pairs={{0,1},{1,2},{2,3},{3,4},{4,5},{5,6},{6,7},{8,9},{9,10},{10,11},{11... | collective-permute-start | bytes 393224 | tf_op jit(solution)/shard_map/ppermute | solution.py:20
  281.5 9.8 %custom-call.10 = f32[1,128,128]{1,2,0:T(8,128)S(1)} custom-call(f32[1,128,128]{2,1,0:T(8,128)S(1)} %fusion.41), custom_call_target="InvertDiagBlocksLowerTriangular" | custom-call | tf_op jit(solution)/shard_map/triangular_solve | solution.py:116
  291.4 2.3 pad_maximum_fusion
  293.9 4.7 %fusion.11 = f32[16,32,1024]{2,1,0:T(8,128)S(1)} fusion(f32[16,32,1024]{2,1,0:T(8,128)S(1)} %copy-done.3, f32[18,34,1024]{2,1,0:T(8,128)S(1)} %pad_maximum_fusion, f32[1,32,1024]{2,1,0:T(8,128)} %collective-permute-done.6, f32[1,32,1024]{2,1,0:T(8,128)} %collective-permute-done.7, f32[18,1,1024]{2,1,0:T(1,128)S(1)} %broadcast_in_dim.30, ...), kind=kLoop, calls=%fused_computation.44 | loop fusion | flops 18874368 | bytes 11231232 | tf_op jit(solution)/shard_map/add | solution.py:63
  300.4 2.4 collective-permute-start.8
  303.9 4.0 collective-permute-done.8
  307.9 11.8 %all_gather.3 = f32[1,2048]{1,0:T(1,128)S(1)} all-gather(f32[1,256]{1,0:T(1,128)S(1)} %collective-permute-done.8), channel_id=1, replica_groups=mesh['wide'=32,'slab'=8] {'slab'}, dimensions={1}, use_global_device_ids=true | all-gather | bytes 9216 | tf_op jit(solution)/shard_map/all_gather | solution.py:105
  319.8 1.7 gather_fusion
  321.7 12.7 %psum.30 = f32[128]{0:T(128)S(1)} all-reduce(f32[128]{0:T(128)S(1)} %convolution_bitcast_fusion.2), channel_id=1, replica_groups=mesh['wide'=32,'slab'=8] {'slab'}, use_global_device_ids=true, to_apply=%region_5.6 | all-reduce | flops 128 | bytes 1024 | tf_op jit(solution)/shard_map/psum | solution.py:111
  334.4 72.9 %psum.31 = f32[128]{0:T(128)S(1)} all-reduce(f32[128]{0:T(128)S(1)} %psum.30), channel_id=1, replica_groups=mesh['wide'=32,'slab'=8] {'wide'}, use_global_device_ids=true, to_apply=%region_6.7 | all-reduce | flops 128 | bytes 1024 | tf_op jit(solution)/shard_map/psum | solution.py:111
  (78 shorter events, 19.8 us)
Async XLA Ops:
  7.2 5.4 %copy-start = (f32[1,256,128]{2,1,0:T(8,128)S(1)}, f32[1,256,128]{2,1,0:T(8,128)}, u32[]{:S(2)}) copy-start(f32[1,256,128]{2,1,0:T(8,128)} %param.12) | copy-start | bytes 393220
  7.2 72.3 %all-reduce.12.cloned.1.call-start = ((), (), s32[]{:S(2)}) async-start(), calls=%async_computation | async-start | bytes 131072 | tf_op jit(solution)/shard_map/psum | solution.py:111
  8.2 214.1 %collective-permute-start = (f32[1,32,1024]{2,1,0:T(8,128)S(1)}, f32[1,32,1024]{2,1,0:T(8,128)S(1)}, u32[]{:S(2)}, u32[]{:S(2)}) collective-permute-start(f32[1,32,1024]{2,1,0:T(8,128)S(1)} %get-tuple-element.16), channel_id=1, source_target_pairs={{1,0},{2,1},{3,2},{4,3},{5,4},{6,5},{7,6},{9,8},{10,9},{11,10},{12... | collective-permute-start | bytes 393224 | tf_op jit(solution)/shard_map/ppermute | solution.py:22
  9.5 212.9 %collective-permute-start.1 = (f32[1,32,1024]{2,1,0:T(8,128)S(1)}, f32[1,32,1024]{2,1,0:T(8,128)S(1)}, u32[]{:S(2)}, u32[]{:S(2)}) collective-permute-start(f32[1,32,1024]{2,1,0:T(8,128)S(1)} %get-tuple-element.15), channel_id=1, source_target_pairs={{0,1},{1,2},{2,3},{3,4},{4,5},{5,6},{6,7},{8,9},{9,10},{10,11},{11... | collective-permute-start | bytes 393224 | tf_op jit(solution)/shard_map/ppermute | solution.py:20
  13.6 207.8 %all-reduce.14.cloned.1.call-start = ((), (), s32[]{:S(2)}) async-start(), calls=%async_computation.1 | async-start | bytes 131072 | tf_op jit(solution)/shard_map/psum | solution.py:111
  223.1 2.6 copy-start.1
  223.1 2.8 copy-start.6
  223.1 2.8 copy-start.11
  225.9 14.0 %copy-start.12 = (f32[128,128]{0,1:T(8,128)S(1)}, f32[128,128]{0,1:T(8,128)}, u32[]{:S(2)}) copy-start(f32[128,128]{0,1:T(8,128)} %all-reduce.14.cloned.1.call-done) | copy-start | bytes 196612
  232.9 1.3 copy-start.4
  235.0 18.2 %collective-permute-start.2 = (f32[1,32,1024]{2,1,0:T(8,128)}, f32[1,32,1024]{2,1,0:T(8,128)S(1)}, u32[]{:S(2)}, u32[]{:S(2)}) collective-permute-start(f32[1,32,1024]{2,1,0:T(8,128)} %get-tuple-element.14), channel_id=1, source_target_pairs={{1,0},{2,1},{3,2},{4,3},{5,4},{6,5},{7,6},{9,8},{10,9},{11,10},{12... | collective-permute-start | bytes 393224 | tf_op jit(solution)/shard_map/ppermute | solution.py:22
  236.2 16.9 %collective-permute-start.3 = (f32[1,32,1024]{2,1,0:T(8,128)}, f32[1,32,1024]{2,1,0:T(8,128)}, u32[]{:S(2)}, u32[]{:S(2)}) collective-permute-start(f32[1,32,1024]{2,1,0:T(8,128)} %get-tuple-element.13), channel_id=1, source_target_pairs={{0,1},{1,2},{2,3},{3,4},{4,5},{5,6},{6,7},{8,9},{9,10},{10,11},{11... | collective-permute-start | bytes 393224 | tf_op jit(solution)/shard_map/ppermute | solution.py:20
  253.1 2.3 copy-start.5
  253.1 2.5 copy-start.7
  260.3 5.2 %collective-permute-start.4 = (f32[1,32,1024]{2,1,0:T(8,128)S(1)}, f32[1,32,1024]{2,1,0:T(8,128)S(1)}, u32[]{:S(2)}, u32[]{:S(2)}) collective-permute-start(f32[1,32,1024]{2,1,0:T(8,128)S(1)} %get-tuple-element.12), channel_id=1, source_target_pairs={{1,0},{2,1},{3,2},{4,3},{5,4},{6,5},{7,6},{9,8},{10,9},{11,10},{12... | collective-permute-start | bytes 393224 | tf_op jit(solution)/shard_map/ppermute | solution.py:22
  261.6 4.0 collective-permute-start.5
  273.8 17.6 %collective-permute-start.6 = (f32[1,32,1024]{2,1,0:T(8,128)}, f32[1,32,1024]{2,1,0:T(8,128)}, u32[]{:S(2)}, u32[]{:S(2)}) collective-permute-start(f32[1,32,1024]{2,1,0:T(8,128)} %get-tuple-element.10), channel_id=1, source_target_pairs={{1,0},{2,1},{3,2},{4,3},{5,4},{6,5},{7,6},{9,8},{10,9},{11,10},{12... | collective-permute-start | bytes 393224 | tf_op jit(solution)/shard_map/ppermute | solution.py:22
  275.1 16.3 %collective-permute-start.7 = (f32[1,32,1024]{2,1,0:T(8,128)}, f32[1,32,1024]{2,1,0:T(8,128)}, u32[]{:S(2)}, u32[]{:S(2)}) collective-permute-start(f32[1,32,1024]{2,1,0:T(8,128)} %get-tuple-element.9), channel_id=1, source_target_pairs={{0,1},{1,2},{2,3},{3,4},{4,5},{5,6},{6,7},{8,9},{9,10},{10,11},{11... | collective-permute-start | bytes 393224 | tf_op jit(solution)/shard_map/ppermute | solution.py:20
  291.4 2.4 copy-start.3
  291.4 2.6 copy-start.8
  300.0 21.5 %copy-start.14 = (s32[1,256]{1,0:T(1,128)S(1)}, s32[1,256]{1,0:T(1,128)}, u32[]{:S(2)}) copy-start(s32[1,256]{1,0:T(1,128)} %param.11) | copy-start | bytes 3076
  300.0 21.6 %copy-start.15 = (f32[1,256]{1,0:T(1,128)S(1)}, f32[1,256]{1,0:T(1,128)}, u32[]{:S(2)}) copy-start(f32[1,256]{1,0:T(1,128)} %param.10) | copy-start | bytes 3076
  300.0 107.7 %copy-start.13 = (f32[1,256,128]{2,1,0:T(8,128)S(1)}, f32[1,256,128]{2,1,0:T(8,128)}, u32[]{:S(2)}) copy-start(f32[1,256,128]{2,1,0:T(8,128)} %param.13) | copy-start | bytes 393220
  300.4 7.5 %collective-permute-start.8 = (f32[1,256]{1,0:T(1,128)S(1)}, f32[1,256]{1,0:T(1,128)S(1)}, u32[]{:S(2)}, u32[]{:S(2)}) collective-permute-start(f32[1,256]{1,0:T(1,128)S(1)} %div.18), channel_id=1, source_target_pairs={{0,128},{8,136},{16,144},{24,152},{32,160},{40,168},{48,176},{56,1... | collective-permute-start | bytes 3080 | tf_op jit(solution)/shard_map/ppermute | solution.py:32
  (3 other events, 3.3 us)
Sparse Core Ops, SparseCore 0:
  13.8 65.7 all-reduce.11
  83.4 138.0 all-reduce.13
